TPU v7x, 32 devices: a whole 2x2x4 slice. The times are simulated.
32 devices in a mesh: hyd: 4 (over y, x), src: 8 (over z, core).
Axes of the slice: x: 2, y: 2, z: 4, core: 2. Of those that a mesh axis runs over, the one named last changes fastest.
Arguments:
- record: float32 [2, 4096, 128], P(None, 'hyd'), may hold values from -6 to 6
- tile_data: bfloat16 [4, 8, 24, 2, 128, 128], P('hyd', 'src'), may hold values from -0.125 to 0.125
- tile_rows: int32 [4, 8, 24], P('hyd', 'src'), may hold values from 0 to 7, as said below
- tile_cols: int32 [4, 8, 24], P('hyd', 'src'), may hold values from 0 to 7, as said below
- tile_counts: int32 [4, 8], P('hyd', 'src'), may hold values from 3 to 24, as said below
Outputs:
- solution: float32 [2, 8192, 128], P(None, 'src')
- residual: float32 [2, 4096, 128], P(None, 'hyd')
Inputs may be any that keep to these rules, and one draw needn't show every extreme that they name: `tile_rows`: together with tile_cols, the 24 slots of one device name different tile pairs. `tile_cols`: column tiles below 4 belong to the upper layer. `tile_counts`: slots at and beyond a device's count hold no tiles of A.
All inputs are finite; a program needn't handle non-finite values.
Results may differ from a plain program's by a relative error of at most 0.014.
Values may be sent and summed in bfloat16 or wider, within the bound.
No kernel may reach another device: no remote copies, remote signals or barrier semaphores. Data moves between devices by JAX's collectives and lax.ppermute only.
A program may use at most 64 MiB of HBM per device.

v0:
```python
import jax
import jax.numpy as jnp
from jax import lax
from jax.sharding import PartitionSpec as P

SRC_DEV = 512
ITERS = 3
EPSILON = 1e-06


def place_tiles(total, products, target, usable):
    for slot in range(products.shape[1]):
        current = lax.dynamic_slice_in_dim(total, target[slot], 1, 1)
        added = current + products[:, slot][:, None] * usable[slot]
        total = lax.dynamic_update_slice_in_dim(total, added, target[slot], 1)
    return total


def tile_forward(tile_group_all, rows_list, cols_list, first_slot, end_slot, vector_b, row_tiles):
    group_slots = 8
    tile_size = tile_group_all.shape[-1]
    shot_count = vector_b.shape[2]
    col_tiles = vector_b.shape[1] // tile_size
    blocks = vector_b.reshape(2, col_tiles, tile_size, shot_count)

    def one_turn(group, total):
        start = group * group_slots
        tile_group = lax.dynamic_slice_in_dim(tile_group_all, start, group_slots, 0)
        col_pick = lax.dynamic_slice_in_dim(cols_list, start, group_slots, 0)
        row_pick = lax.dynamic_slice_in_dim(rows_list, start, group_slots, 0)
        slot_ids = start + jnp.arange(group_slots)
        usable = ((slot_ids >= first_slot) & (slot_ids < end_slot)).astype(jnp.float32)
        chosen = jnp.take(blocks, col_pick, axis=1)
        real_part = jnp.einsum(
            "gij,gjn->gin", tile_group[:, 0], chosen[0], preferred_element_type=jnp.float32
        ) - jnp.einsum(
            "gij,gjn->gin", tile_group[:, 1], chosen[1], preferred_element_type=jnp.float32
        )
        imag_part = jnp.einsum(
            "gij,gjn->gin", tile_group[:, 0], chosen[1], preferred_element_type=jnp.float32
        ) + jnp.einsum(
            "gij,gjn->gin", tile_group[:, 1], chosen[0], preferred_element_type=jnp.float32
        )
        return place_tiles(total, jnp.stack([real_part, imag_part]), row_pick, usable)

    empty = jnp.zeros((2, row_tiles, tile_size, shot_count), jnp.float32)
    result = lax.fori_loop(
        first_slot // group_slots, (end_slot + group_slots - 1) // group_slots, one_turn, empty
    )
    return result.reshape(2, row_tiles * tile_size, shot_count)


def tile_adjoint(tile_group_all, rows_list, cols_list, first_slot, end_slot, residual_b, col_tiles):
    group_slots = 8
    tile_size = tile_group_all.shape[-1]
    shot_count = residual_b.shape[2]
    row_tiles = residual_b.shape[1] // tile_size
    blocks = residual_b.reshape(2, row_tiles, tile_size, shot_count)

    def one_turn(group, total):
        start = group * group_slots
        tile_group = lax.dynamic_slice_in_dim(tile_group_all, start, group_slots, 0)
        col_pick = lax.dynamic_slice_in_dim(cols_list, start, group_slots, 0)
        row_pick = lax.dynamic_slice_in_dim(rows_list, start, group_slots, 0)
        slot_ids = start + jnp.arange(group_slots)
        usable = ((slot_ids >= first_slot) & (slot_ids < end_slot)).astype(jnp.float32)
        chosen = jnp.take(blocks, row_pick, axis=1)
        real_part = jnp.einsum(
            "gji,gjn->gin", tile_group[:, 0], chosen[0], preferred_element_type=jnp.float32
        ) + jnp.einsum(
            "gji,gjn->gin", tile_group[:, 1], chosen[1], preferred_element_type=jnp.float32
        )
        imag_part = jnp.einsum(
            "gji,gjn->gin", tile_group[:, 0], chosen[1], preferred_element_type=jnp.float32
        ) - jnp.einsum(
            "gji,gjn->gin", tile_group[:, 1], chosen[0], preferred_element_type=jnp.float32
        )
        return place_tiles(total, jnp.stack([real_part, imag_part]), col_pick, usable)

    empty = jnp.zeros((2, col_tiles, tile_size, shot_count), jnp.float32)
    result = lax.fori_loop(
        first_slot // group_slots, (end_slot + group_slots - 1) // group_slots, one_turn, empty
    )
    return result.reshape(2, col_tiles * tile_size, shot_count)


def body(record, tile_data, tile_rows, tile_cols, tile_counts):
    own_tiles = tile_data[0, 0]
    own_rows = tile_rows[0, 0]
    own_cols = tile_cols[0, 0]
    own_count = tile_counts[0, 0]
    tile_size = own_tiles.shape[-1]
    row_tiles = record.shape[1] // tile_size
    col_tiles = 2 * SRC_DEV // tile_size

    def gradient_of(residual_b):
        partial_value = tile_adjoint(
            own_tiles, own_rows, own_cols, 0, own_count, residual_b, col_tiles
        )
        gradient = lax.psum(partial_value, "hyd")
        squares = lax.psum(jnp.sum(gradient * gradient, axis=(0, 1)), "src")
        return (gradient, squares)

    residual = record
    gradient, gamma_now = gradient_of(record.astype(jnp.bfloat16))
    direction = gradient
    solution = jnp.zeros_like(gradient)
    for step_index in range(ITERS):
        direction_b = direction.astype(jnp.bfloat16)
        forward_partial_value = tile_forward(
            own_tiles, own_rows, own_cols, 0, own_count, direction_b, row_tiles
        )
        image = lax.psum(forward_partial_value, "src")
        image_sq = lax.psum(jnp.sum(image * image, axis=(0, 1)), "hyd")
        image, image_sq = (image, image_sq)
        alpha_step = gamma_now / (image_sq + EPSILON)
        solution = solution + alpha_step * direction
        residual = residual - alpha_step * image
        if step_index + 1 < ITERS:
            residual_b = residual.astype(jnp.bfloat16)
            gradient, gamma_next = gradient_of(residual_b)
            direction = gradient + gamma_next / (gamma_now + EPSILON) * direction
            gamma_now = gamma_next
    return (solution, residual)


def solution(mesh):
    in_specs = (
        P(None, "hyd", None),
        P("hyd", "src", None, None, None, None),
        P("hyd", "src", None),
        P("hyd", "src", None),
        P("hyd", "src"),
    )
    out_specs = (P(None, "src", None), P(None, "hyd", None))
    return jax.shard_map(body, mesh=mesh, in_specs=in_specs, out_specs=out_specs, check_vma=False)
```

profile of v0, /device:TPU:0, one launch (start us, length us, event | category | flops | bytes accessed | tf_op | source)
XLA Modules:
  0.0 1104.4 jit_solution(888676539581461893)
XLA Ops:
  7.9 2.7 copy.18
  11.3 28.1 %while.60 = (s32[]{:T(128)}, f32[2,8,128,128]{3,2,1,0:T(8,128)S(1)}, s32[]{:T(128)}, s32[24]{0:T(128)S(1)}, bf16[24,2,128,128]{2,3,0,1:T(8,128)(2,1)}, /*index=5...) while((s32[]{:T(128)}, ...), condition=%wide.region_1.3_spmd, body=%wide.region_0.2_spmd.sunk | while | flops 135529568 | bytes 17830816 | solution.py:81
  41.9 108.4 %all-reduce.7.cloned.1.call-done = f32[2,1024,128]{2,1,0:T(8,128)} async-done(((f32[2,1024,128]{2,1,0:T(8,128)}), f32[2,1024,128]{2,1,0:T(8,128)}) %all-reduce.7.cloned.1.call-update) | async-done | bytes 1048592 | tf_op jit(solution)/shard_map/psum | solution.py:100
  150.3 2.5 multiply_reduce_fusion.5
  153.9 38.0 %while.61 = (s32[]{:T(128)}, f32[2,8,128,128]{3,2,1,0:T(8,128)}, s32[]{:T(128)}, s32[24]{0:T(128)S(1)}, bf16[24,2,128,128]{3,2,0,1:T(8,128)(2,1)S(1)}, /*index=5...) while((s32[]{:T(128)}, f32[2,8,128,128]{3,2,1,0:T(8,128)}, ...), condition=%wide.region_6.8_spmd, body=%wide.region_5.7_spmd.sunk | while | flops 135529568 | bytes 17834880 | solution.py:47
  160.6 2.3 fusion.368
  164.8 2.2 fusion.369
  177.4 2.2 fusion.372
  185.8 2.3 fusion.374
  192.0 92.6 %psum.85 = f32[128]{0:T(128)S(1)} all-reduce(f32[128]{0:T(128)S(1)} %get-tuple-element.527), channel_id=1, replica_groups=mesh['hyd'=4,'src'=8] {'src'}, use_global_device_ids=true, to_apply=%region_4.6 | all-reduce | flops 128 | bytes 1024 | tf_op jit(solution)/shard_map/psum | solution.py:101
  284.6 42.1 %all-reduce.9.cloned.1.call-done = f32[2,1024,128]{2,1,0:T(8,128)} async-done(((f32[2,1024,128]{2,1,0:T(8,128)}), f32[2,1024,128]{2,1,0:T(8,128)}) %all-reduce.9.cloned.1.call-update) | async-done | bytes 1048592 | tf_op jit(solution)/shard_map/psum | solution.py:113
  328.2 9.8 psum.87
  341.2 41.8 %while.62 = (s32[]{:T(128)}, f32[2,8,128,128]{3,2,1,0:T(8,128)}, s32[]{:T(128)}, s32[24]{0:T(128)S(1)}, bf16[24,2,128,128]{2,3,0,1:T(8,128)(2,1)}, /*index=5*/s3...) while((s32[]{:T(128)}, f32[2,8,128,128]{3,2,1,0:T(8,128)}, ...), condition=%wide.region_11.13_spmd, body=%wide.region_10.12_spmd.sunk | while | flops 135529568 | bytes 17834880 | solution.py:81
  351.6 2.3 fusion.383
  355.9 2.2 fusion.384
  368.4 2.2 fusion.387
  376.9 2.3 fusion.389
  383.1 132.6 %all-reduce.11.cloned.1.call-done = f32[2,1024,128]{2,1,0:T(8,128)} async-done(((f32[2,1024,128]{2,1,0:T(8,128)}), f32[2,1024,128]{2,1,0:T(8,128)}) %all-reduce.11.cloned.1.call-update) | async-done | bytes 1048592 | tf_op jit(solution)/shard_map/psum | solution.py:100
  517.2 16.2 %psum.89 = f32[128]{0:T(128)S(1)} all-reduce(f32[128]{0:T(128)S(1)} %multiply_reduce_fusion.3), channel_id=1, replica_groups=mesh['hyd'=4,'src'=8] {'src'}, use_global_device_ids=true, to_apply=%region_14.16 | all-reduce | flops 128 | bytes 1024 | tf_op jit(solution)/shard_map/psum | solution.py:101
  536.6 38.0 %while.63 = (s32[]{:T(128)}, f32[2,8,128,128]{3,2,1,0:T(8,128)}, s32[]{:T(128)}, s32[24]{0:T(128)S(1)}, bf16[24,2,128,128]{3,2,0,1:T(8,128)(2,1)S(1)}, /*index=5...) while((s32[]{:T(128)}, f32[2,8,128,128]{3,2,1,0:T(8,128)}, ...), condition=%wide.region_16.18_spmd, body=%wide.region_15.17_spmd.sunk | while | flops 135529568 | bytes 17834880 | solution.py:47
  543.6 2.2 fusion.398
  547.8 2.2 fusion.399
  552.0 2.2 fusion.400
  556.1 2.3 fusion.401
  564.2 2.2 fusion.403
  572.3 2.3 fusion.405
  574.7 131.5 %all-reduce.13.cloned.1.call-done = f32[2,1024,128]{2,1,0:T(8,128)} async-done(((f32[2,1024,128]{2,1,0:T(8,128)}), f32[2,1024,128]{2,1,0:T(8,128)}) %all-reduce.13.cloned.1.call-update) | async-done | bytes 1048592 | tf_op jit(solution)/shard_map/psum | solution.py:113
  707.7 9.8 psum.91
  717.5 2.9 fusion.243
  721.4 41.1 %while.64 = (s32[]{:T(128)}, f32[2,8,128,128]{3,2,1,0:T(8,128)}, s32[]{:T(128)}, s32[24]{0:T(128)S(1)}, bf16[24,2,128,128]{2,3,0,1:T(8,128)(2,1)}, /*index=5*/s3...) while((s32[]{:T(128)}, f32[2,8,128,128]{3,2,1,0:T(8,128)}, ...), condition=%wide.region_21.23_spmd, body=%wide.region_20.22_spmd.sunk | while | flops 135529568 | bytes 17834880 | solution.py:81
  732.0 2.2 fusion.413
  736.0 2.3 fusion.414
  740.0 2.2 fusion.415
  748.1 2.2 fusion.417
  756.1 2.3 fusion.419
  760.3 2.2 fusion.420
  762.6 131.3 %all-reduce.15.cloned.1.call-done = f32[2,1024,128]{2,1,0:T(8,128)} async-done(((f32[2,1024,128]{2,1,0:T(8,128)}), f32[2,1024,128]{2,1,0:T(8,128)}) %all-reduce.15.cloned.1.call-update) | async-done | bytes 1048592 | tf_op jit(solution)/shard_map/psum | solution.py:100
  895.4 16.2 %psum.93 = f32[128]{0:T(128)S(1)} all-reduce(f32[128]{0:T(128)S(1)} %multiply_reduce_fusion.1), channel_id=1, replica_groups=mesh['hyd'=4,'src'=8] {'src'}, use_global_device_ids=true, to_apply=%region_24.26 | all-reduce | flops 128 | bytes 1024 | tf_op jit(solution)/shard_map/psum | solution.py:101
  911.6 2.5 fusion.240
  915.2 37.3 %while.65 = (s32[]{:T(128)}, f32[2,8,128,128]{3,2,1,0:T(8,128)}, s32[]{:T(128)}, s32[24]{0:T(128)S(1)}, bf16[24,2,128,128]{3,2,0,1:T(8,128)(2,1)S(1)}, /*index=5...) while((s32[]{:T(128)}, f32[2,8,128,128]{3,2,1,0:T(8,128)}, ...), condition=%wide.region_26.28_spmd, body=%wide.region_25.27_spmd.sunk | while | flops 135529568 | bytes 17834880 | solution.py:47
  921.9 2.2 fusion.428
  926.0 2.3 fusion.429
  930.0 2.2 fusion.430
  938.0 2.2 fusion.432
  946.1 2.3 fusion.434
  952.5 130.2 %all-reduce.17.cloned.1.call-done = f32[2,1024,128]{2,1,0:T(8,128)} async-done(((f32[2,1024,128]{2,1,0:T(8,128)}), f32[2,1024,128]{2,1,0:T(8,128)}) %all-reduce.17.cloned.1.call-update) | async-done | bytes 1048592 | tf_op jit(solution)/shard_map/psum | solution.py:113
  1084.2 9.8 psum.95
  1094.0 3.6 multiply_subtract_fusion
  (141 shorter events, 97.7 us)
Async XLA Ops:
  7.2 143.2 %all-reduce.7.cloned.1.call-start = ((), (), s32[]{:S(2)}) async-start(), calls=%async_computation | async-start | bytes 2097152 | tf_op jit(solution)/shard_map/psum | solution.py:100
  7.9 2.7 copy-start.5
  10.6 0.7 copy-start.8
  10.6 0.7 copy-start.9
  39.3 1.0 copy-start
  40.3 286.4 %all-reduce.9.cloned.1.call-start = ((), (), s32[]{:S(2)}) async-start(), calls=%async_computation.1 | async-start | bytes 2097152 | tf_op jit(solution)/shard_map/psum | solution.py:113
  191.9 146.1 %copy-start.6 = (f32[2,1024,128]{2,1,0:T(8,128)S(1)}, f32[2,1024,128]{2,1,0:T(8,128)}, u32[]{:S(2)}) copy-start(f32[2,1024,128]{2,1,0:T(8,128)} %param.19) | copy-start | bytes 3145732
  192.0 323.8 %all-reduce.11.cloned.1.call-start = ((), (), s32[]{:S(2)}) async-start(), calls=%async_computation.2 | async-start | bytes 2097152 | tf_op jit(solution)/shard_map/psum | solution.py:100
  383.0 150.4 %copy-start.1 = (f32[2,1024,128]{2,1,0:T(8,128)S(1)}, f32[2,1024,128]{2,1,0:T(8,128)}, u32[]{:S(2)}) copy-start(f32[2,1024,128]{2,1,0:T(8,128)} %all-reduce.7.cloned.1.call-done) | copy-start | bytes 3145732
  383.0 323.1 %all-reduce.13.cloned.1.call-start = ((), (), s32[]{:S(2)}) async-start(), calls=%async_computation.3 | async-start | bytes 2097152 | tf_op jit(solution)/shard_map/psum | solution.py:113
  574.6 142.8 %copy-start.7 = (f32[2,1024,128]{2,1,0:T(8,128)S(1)}, f32[2,1024,128]{2,1,0:T(8,128)}, u32[]{:S(2)}) copy-start(f32[2,1024,128]{2,1,0:T(8,128)} %param.19) | copy-start | bytes 3145732
  574.6 319.2 %all-reduce.15.cloned.1.call-start = ((), (), s32[]{:S(2)}) async-start(), calls=%async_computation.4 | async-start | bytes 2097152 | tf_op jit(solution)/shard_map/psum | solution.py:100
  762.5 149.0 %copy-start.2 = (f32[2,1024,128]{2,1,0:T(8,128)S(1)}, f32[2,1024,128]{2,1,0:T(8,128)}, u32[]{:S(2)}) copy-start(f32[2,1024,128]{2,1,0:T(8,128)} %all-reduce.7.cloned.1.call-done) | copy-start | bytes 3145732
  762.6 320.1 %all-reduce.17.cloned.1.call-start = ((), (), s32[]{:S(2)}) async-start(), calls=%async_computation.5 | async-start | bytes 2097152 | tf_op jit(solution)/shard_map/psum | solution.py:113
  952.5 141.5 %copy-start.3 = (f32[2,1024,128]{2,1,0:T(8,128)S(1)}, f32[2,1024,128]{2,1,0:T(8,128)}, u32[]{:S(2)}) copy-start(f32[2,1024,128]{2,1,0:T(8,128)} %all-reduce.7.cloned.1.call-done) | copy-start | bytes 3145732
  952.5 141.5 %copy-start.4 = (f32[2,1024,128]{2,1,0:T(8,128)S(1)}, f32[2,1024,128]{2,1,0:T(8,128)}, u32[]{:S(2)}) copy-start(f32[2,1024,128]{2,1,0:T(8,128)} %all-reduce.11.cloned.1.call-done) | copy-start | bytes 3145732
Sparse Core Ops, SparseCore 0:
  40.4 109.8 all-reduce.6
  192.1 134.5 all-reduce.8
  383.1 132.5 all-reduce.10
  574.8 131.3 all-reduce.12
  762.7 131.1 all-reduce.14
  952.6 130.0 all-reduce.16
where the time goes:
time: 1110 us; the launch traced here: 1100 us
  waiting for transfers between devices  676 us (61%)
  blocking collectives  154 us (14%)
  other arithmetic  122 us (11%)
  loops' own time  91.6 us (8%)
  local copies, waits for them, and re-layouts  29 us (3%)
  matrix products  16.7 us (2%)
  between operations  14.9 us (1%)
    psum x3, waiting for transfers between devices, gradient_of(): gradient = lax.psum(partial_value, 'hyd')  372 us
    psum x3, waiting for transfers between devices, body(): image = lax.psum(forward_partial_value, 'src')  304 us
    psum x3, blocking collectives, gradient_of(): squares = lax.psum(jnp.sum(gradient * gradient, axis=(0, 1)), 'src')  125 us
    dynamic_update_slice x48, other arithmetic, place_tiles(): total = lax.dynamic_update_slice_in_dim(total, added, target[slot], 1)  93.1 us
    another operation x3, loops' own time, tile_forward(): lax.fori_loop(first_slot // group_slots, (end_slot + group_slots - 1) //...  45.9 us
    another operation x3, loops' own time, tile_adjoint(): lax.fori_loop(first_slot // group_slots, (end_slot + group_slots - 1) //...  45.7 us
    psum x3, blocking collectives, body(): image_sq = lax.psum(jnp.sum(image * image, axis=(0, 1)), 'hyd')  29.3 us
  transfers between devices with their start and end apart: 6, of which 6 were waited for; matrix products, arithmetic and copies ran while one was open for 0% of the time, Pallas kernels for 0%

commit v1 on v0

--- a/solution.py
+++ b/solution.py
@@ -6,6 +6,12 @@
 SRC_DEV = 512
 ITERS = 3
 EPSILON = 1e-06
+
+
+def gather_and_add(array, axis):
+    parts = lax.all_gather(array, axis, axis=0, tiled=False)
+    acc = parts.sum(axis=0)
+    return acc
 
 
 def place_tiles(total, products, target, usable):
@@ -110,7 +116,7 @@
         forward_partial_value = tile_forward(
             own_tiles, own_rows, own_cols, 0, own_count, direction_b, row_tiles
         )
-        image = lax.psum(forward_partial_value, "src")
+        image = gather_and_add(forward_partial_value, "src")
         image_sq = lax.psum(jnp.sum(image * image, axis=(0, 1)), "hyd")
         image, image_sq = (image, image_sq)
         alpha_step = gamma_now / (image_sq + EPSILON)

time: 1110 us -> 1190 us (1.072)
  waiting for transfers between devices: 676 us -> 739 us
  other arithmetic: 122 us -> 134 us
    all_gather x0 -> x3, waiting for transfers between devices: none -> 371 us  [gather_and_add(): parts = lax.all_gather(array, axis, axis=0, tiled=False)]
    psum x3 -> x0, waiting for transfers between devices: 304 us -> none  [body(): image = lax.psum(forward_partial_value, 'src')]
    reduce_sum x0 -> x3, other arithmetic: none -> 13.7 us  [gather_and_add(): acc = parts.sum(axis=0)]
where the time goes in v1:
time: 1190 us; the launch traced here: 1180 us
  waiting for transfers between devices  739 us (62%)
  blocking collectives  154 us (13%)
  other arithmetic  134 us (11%)
  loops' own time  90.2 us (8%)
  local copies, waits for them, and re-layouts  28.9 us (2%)
  matrix products  16.7 us (1%)
  between operations  14.9 us (1%)
    all_gather x3, waiting for transfers between devices, gather_and_add(): parts = lax.all_gather(array, axis, axis=0, tiled=False)  371 us
    psum x3, waiting for transfers between devices, gradient_of(): gradient = lax.psum(partial_value, 'hyd')  367 us
    psum x3, blocking collectives, gradient_of(): squares = lax.psum(jnp.sum(gradient * gradient, axis=(0, 1)), 'src')  124 us
    dynamic_update_slice x48, other arithmetic, place_tiles(): total = lax.dynamic_update_slice_in_dim(total, added, target[slot], 1)  93.2 us
    another operation x3, loops' own time, tile_forward(): lax.fori_loop(first_slot // group_slots, (end_slot + group_slots - 1) //...  45.1 us
    another operation x3, loops' own time, tile_adjoint(): lax.fori_loop(first_slot // group_slots, (end_slot + group_slots - 1) //...  45 us
    psum x3, blocking collectives, body(): image_sq = lax.psum(jnp.sum(image * image, axis=(0, 1)), 'hyd')  29.5 us
  transfers between devices with their start and end apart: 6, of which 6 were waited for; matrix products, arithmetic and copies ran while one was open for 0% of the time, Pallas kernels for 0%

profile of v1, /device:TPU:0, one launch (start us, length us, event | category | flops | bytes accessed | tf_op | source)
XLA Modules:
  0.0 1177.6 jit_solution(13305303398001013003)
XLA Ops:
  7.9 2.7 copy.28
  11.3 27.7 %while.60 = (s32[]{:T(128)}, f32[2,8,128,128]{3,2,1,0:T(8,128)S(1)}, s32[]{:T(128)}, s32[24]{0:T(128)S(1)}, bf16[24,2,128,128]{2,3,0,1:T(8,128)(2,1)}, /*index=5...) while((s32[]{:T(128)}, ...), condition=%wide.region_1.3_spmd, body=%wide.region_0.2_spmd.sunk | while | flops 135529568 | bytes 17830816 | solution.py:87
  41.7 107.7 %all-reduce.4.cloned.1.call-done = f32[2,1024,128]{2,1,0:T(8,128)} async-done(((f32[2,1024,128]{2,1,0:T(8,128)}), f32[2,1024,128]{2,1,0:T(8,128)}) %all-reduce.4.cloned.1.call-update) | async-done | bytes 1048592 | tf_op jit(solution)/shard_map/psum | solution.py:106
  149.4 2.6 multiply_reduce_fusion.5
  153.1 37.5 %while.61 = (s32[]{:T(128)}, f32[2,8,128,128]{3,2,1,0:T(8,128)}, s32[]{:T(128)}, s32[24]{0:T(128)S(1)}, bf16[24,2,128,128]{3,2,0,1:T(8,128)(2,1)S(1)}, /*index=5...) while((s32[]{:T(128)}, f32[2,8,128,128]{3,2,1,0:T(8,128)}, ...), condition=%wide.region_6.8_spmd, body=%wide.region_5.7_spmd.sunk | while | flops 135529568 | bytes 17834880 | solution.py:53
  164.0 2.3 fusion.369
  172.0 2.2 fusion.371
  180.1 2.2 fusion.373
  188.4 2.3 fusion.375
  190.7 91.9 %psum.64 = f32[128]{0:T(128)S(1)} all-reduce(f32[128]{0:T(128)S(1)} %get-tuple-element.551), channel_id=1, replica_groups=mesh['hyd'=4,'src'=8] {'src'}, use_global_device_ids=true, to_apply=%region_4.6 | all-reduce | flops 128 | bytes 1024 | tf_op jit(solution)/shard_map/psum | solution.py:107
  282.6 64.7 %all-gather.4.cloned.1.call-done = f32[8,2,1024,128]{3,2,1,0:T(8,128)} async-done(((f32[1,2,1024,128]{3,2,1,0:T(8,128)}), f32[8,2,1024,128]{3,2,1,0:T(8,128)}) %all-gather.4.cloned.1.call-update) | async-done | bytes 8388624 | tf_op jit(solution)/shard_map/all_gather | solution.py:12
  347.3 3.9 reduce_sum.82
  351.5 9.8 psum.65
  364.5 41.4 %while.62 = (s32[]{:T(128)}, f32[2,8,128,128]{3,2,1,0:T(8,128)}, s32[]{:T(128)}, s32[24]{0:T(128)S(1)}, bf16[24,2,128,128]{2,3,0,1:T(8,128)(2,1)}, /*index=5*/s3...) while((s32[]{:T(128)}, f32[2,8,128,128]{3,2,1,0:T(8,128)}, ...), condition=%wide.region_11.13_spmd, body=%wide.region_10.12_spmd.sunk | while | flops 135529568 | bytes 17834880 | solution.py:87
  379.2 2.3 fusion.384
  387.3 2.2 fusion.386
  395.4 2.2 fusion.388
  403.6 2.3 fusion.390
  405.9 130.1 %all-reduce.6.cloned.1.call-done = f32[2,1024,128]{2,1,0:T(8,128)} async-done(((f32[2,1024,128]{2,1,0:T(8,128)}), f32[2,1024,128]{2,1,0:T(8,128)}) %all-reduce.6.cloned.1.call-update) | async-done | bytes 1048592 | tf_op jit(solution)/shard_map/psum | solution.py:106
  537.5 16.2 %psum.67 = f32[128]{0:T(128)S(1)} all-reduce(f32[128]{0:T(128)S(1)} %multiply_reduce_fusion.3), channel_id=1, replica_groups=mesh['hyd'=4,'src'=8] {'src'}, use_global_device_ids=true, to_apply=%region_14.16 | all-reduce | flops 128 | bytes 1024 | tf_op jit(solution)/shard_map/psum | solution.py:107
  556.9 37.4 %while.63 = (s32[]{:T(128)}, f32[2,8,128,128]{3,2,1,0:T(8,128)}, s32[]{:T(128)}, s32[24]{0:T(128)S(1)}, bf16[24,2,128,128]{3,2,0,1:T(8,128)(2,1)S(1)}, /*index=5...) while((s32[]{:T(128)}, f32[2,8,128,128]{3,2,1,0:T(8,128)}, ...), condition=%wide.region_16.18_spmd, body=%wide.region_15.17_spmd.sunk | while | flops 135529568 | bytes 17834880 | solution.py:53
  563.7 2.2 fusion.398
  571.6 2.3 fusion.400
  580.1 2.2 fusion.402
  588.0 2.2 fusion.404
  594.4 153.0 %all-gather.6.cloned.1.call-done = f32[8,2,1024,128]{3,2,1,0:T(8,128)} async-done(((f32[1,2,1024,128]{3,2,1,0:T(8,128)}), f32[8,2,1024,128]{3,2,1,0:T(8,128)}) %all-gather.6.cloned.1.call-update) | async-done | bytes 8388624 | tf_op jit(solution)/shard_map/all_gather | solution.py:12
  747.4 4.9 reduce_sum.85
  753.9 9.8 psum.68
  763.7 2.9 fusion.243
  767.6 41.2 %while.64 = (s32[]{:T(128)}, f32[2,8,128,128]{3,2,1,0:T(8,128)}, s32[]{:T(128)}, s32[24]{0:T(128)S(1)}, bf16[24,2,128,128]{2,3,0,1:T(8,128)(2,1)}, /*index=5*/s3...) while((s32[]{:T(128)}, f32[2,8,128,128]{3,2,1,0:T(8,128)}, ...), condition=%wide.region_21.23_spmd, body=%wide.region_20.22_spmd.sunk | while | flops 135529568 | bytes 17834880 | solution.py:87
  778.2 2.2 fusion.413
  786.1 2.3 fusion.415
  794.6 2.2 fusion.417
  802.5 2.2 fusion.419
  808.9 129.7 %all-reduce.8.cloned.1.call-done = f32[2,1024,128]{2,1,0:T(8,128)} async-done(((f32[2,1024,128]{2,1,0:T(8,128)}), f32[2,1024,128]{2,1,0:T(8,128)}) %all-reduce.8.cloned.1.call-update) | async-done | bytes 1048592 | tf_op jit(solution)/shard_map/psum | solution.py:106
  940.1 16.2 %psum.70 = f32[128]{0:T(128)S(1)} all-reduce(f32[128]{0:T(128)S(1)} %multiply_reduce_fusion.1), channel_id=1, replica_groups=mesh['hyd'=4,'src'=8] {'src'}, use_global_device_ids=true, to_apply=%region_24.26 | all-reduce | flops 128 | bytes 1024 | tf_op jit(solution)/shard_map/psum | solution.py:107
  956.3 2.5 fusion.240
  959.9 37.5 %while.65 = (s32[]{:T(128)}, f32[2,8,128,128]{3,2,1,0:T(8,128)}, s32[]{:T(128)}, s32[24]{0:T(128)S(1)}, bf16[24,2,128,128]{3,2,0,1:T(8,128)(2,1)S(1)}, /*index=5...) while((s32[]{:T(128)}, f32[2,8,128,128]{3,2,1,0:T(8,128)}, ...), condition=%wide.region_26.28_spmd, body=%wide.region_25.27_spmd.sunk | while | flops 135529568 | bytes 17834880 | solution.py:53
  966.8 2.2 fusion.428
  970.7 2.2 fusion.429
  978.8 2.2 fusion.431
  986.9 2.2 fusion.433
  991.0 2.2 fusion.434
  995.1 2.3 fusion.435
  997.4 153.4 %all-gather.8.cloned.1.call-done = f32[8,2,1024,128]{3,2,1,0:T(8,128)} async-done(((f32[1,2,1024,128]{3,2,1,0:T(8,128)}), f32[8,2,1024,128]{3,2,1,0:T(8,128)}) %all-gather.8.cloned.1.call-update) | async-done | bytes 8388624 | tf_op jit(solution)/shard_map/all_gather | solution.py:12
  1150.8 4.9 reduce_sum.88
  1157.4 9.8 psum.71
  1167.2 3.6 multiply_subtract_fusion
  (144 shorter events, 103.3 us)
Async XLA Ops:
  7.2 142.2 %all-reduce.4.cloned.1.call-start = ((), (), s32[]{:S(2)}) async-start(), calls=%async_computation | async-start | bytes 2097152 | tf_op jit(solution)/shard_map/psum | solution.py:106
  7.9 2.8 copy-start.7
  10.6 0.7 copy-start.8
  10.6 0.7 copy-start.9
  39.0 1.0 copy-start
  40.0 307.3 %all-gather.4.cloned.1.call-start = ((), (), s32[]{:S(2)}) async-start(), calls=%async_computation.1 | async-start | bytes 9437184 | tf_op jit(solution)/shard_map/all_gather | solution.py:12
  190.7 345.4 %all-reduce.6.cloned.1.call-start = ((), (), s32[]{:S(2)}) async-start(), calls=%async_computation.2 | async-start | bytes 2097152 | tf_op jit(solution)/shard_map/psum | solution.py:106
  351.2 12.2 %copy-start.1 = (f32[2,1024,128]{2,1,0:T(8,128)}, f32[2,1024,128]{2,1,0:T(8,128)S(1)}, u32[]{:S(2)}) copy-start(f32[2,1024,128]{2,1,0:T(8,128)S(1)} %reduce_sum.82) | copy-start | bytes 3145732
  405.9 147.9 %copy-start.3 = (f32[2,1024,128]{2,1,0:T(8,128)S(1)}, f32[2,1024,128]{2,1,0:T(8,128)}, u32[]{:S(2)}) copy-start(f32[2,1024,128]{2,1,0:T(8,128)} %all-reduce.4.cloned.1.call-done) | copy-start | bytes 3145732
  405.9 341.5 %all-gather.6.cloned.1.call-start = ((), (), s32[]{:S(2)}) async-start(), calls=%async_computation.3 | async-start | bytes 9437184 | tf_op jit(solution)/shard_map/all_gather | solution.py:12
  594.3 344.3 %all-reduce.8.cloned.1.call-start = ((), (), s32[]{:S(2)}) async-start(), calls=%async_computation.4 | async-start | bytes 2097152 | tf_op jit(solution)/shard_map/psum | solution.py:106
  752.3 11.4 copy-start.2
  808.8 147.5 %copy-start.4 = (f32[2,1024,128]{2,1,0:T(8,128)S(1)}, f32[2,1024,128]{2,1,0:T(8,128)}, u32[]{:S(2)}) copy-start(f32[2,1024,128]{2,1,0:T(8,128)} %all-reduce.4.cloned.1.call-done) | copy-start | bytes 3145732
  808.8 342.0 %all-gather.8.cloned.1.call-start = ((), (), s32[]{:S(2)}) async-start(), calls=%async_computation.5 | async-start | bytes 9437184 | tf_op jit(solution)/shard_map/all_gather | solution.py:12
  1150.8 16.4 %copy-start.6 = (f32[2,1024,128]{2,1,0:T(8,128)S(1)}, f32[2,1024,128]{2,1,0:T(8,128)}, u32[]{:S(2)}) copy-start(f32[2,1024,128]{2,1,0:T(8,128)} %all-reduce.6.cloned.1.call-done) | copy-start | bytes 3145732
  1155.8 11.5 copy-start.5
Sparse Core Ops, SparseCore 0:
  40.1 109.1 all-reduce.3
  190.8 156.4 all-gather.3
  406.0 129.9 all-reduce.5
  594.4 152.9 all-gather.5
  809.0 129.5 all-reduce.7
  997.5 153.2 all-gather.7
